TPU v7x, 32 devices: a whole 2x2x4 slice. The times are simulated.
32 devices in a mesh: dp: 16 (over z, x, core), tensor: 2 (over y).
Axes of the slice: x: 2, y: 2, z: 4, core: 2. Of those that a mesh axis runs over, the one named last changes fastest.
Arguments:
- tokens: bfloat16 [4096, 8192], P('dp', 'tensor'), may hold values from -6 to 6
- out_grad: bfloat16 [4096, 2, 256], P('dp', 'tensor'), may hold values from -2 to 2
- active: int32 [16, 2, 2], P('dp', 'tensor'), may hold values from 0 to 112, as said below
- w_gate: bfloat16 [8192, 28672], P('dp', 'tensor'), may hold values from -0.0625 to 0.0625
- w_up: bfloat16 [8192, 28672], P('dp', 'tensor'), may hold values from -0.0625 to 0.0625
Outputs:
- input_grad: bfloat16 [4096, 8192], P('dp', 'tensor')
- gate_weight_grad: bfloat16 [8192, 28672], P('dp', 'tensor')
- up_weight_grad: bfloat16 [8192, 28672], P('dp', 'tensor')
Inputs may be any that keep to these rules, and one draw needn't show every extreme that they name: `active`: each entry is a block number of the shard or 112 for an empty slot. In every tile and shard the live entries come first, are distinct and number at least one; in every tile some shard has all 2 slots live.
All inputs are finite; a program needn't handle non-finite values.
Results may differ from a plain program's by a relative error of at most 0.014.
Values may be sent and summed in bfloat16 or wider, within the bound.
No kernel may reach another device: no remote copies, remote signals or barrier semaphores. Data moves between devices by JAX's collectives and lax.ppermute only.
A program may use at most 128 MiB of HBM per device.

v0:
```python
import jax
import jax.numpy as jnp
from jax import lax
from jax.sharding import PartitionSpec as P

BLOCK = 128
TILE = 256
CAP = 2


def per_device(tokens, out_grad, active, w_gate, w_up):
    row_count = tokens.shape[0]
    tiles_here = active.shape[0]
    blocks = w_gate.shape[1] // BLOCK
    rows_local = w_gate.shape[0]
    gathered = lax.all_gather(tokens, "tensor", axis=1, tiled=True)
    full_width = gathered.shape[1]
    listed = lax.all_gather(active, "dp", axis=0, tiled=True)
    peer_count = lax.axis_size("dp")
    slot_count = tiles_here * CAP
    wanted = jnp.minimum(listed.reshape(peer_count, slot_count), blocks - 1)
    gate_send = jnp.take(w_gate.reshape(rows_local, blocks, BLOCK), wanted, axis=1).reshape(
        rows_local, peer_count, slot_count * BLOCK
    )
    up_send = jnp.take(w_up.reshape(rows_local, blocks, BLOCK), wanted, axis=1).reshape(
        rows_local, peer_count, slot_count * BLOCK
    )
    gate_cols, up_cols = (
        lax.all_to_all(gate_send, "dp", split_axis=1, concat_axis=0, tiled=True),
        lax.all_to_all(up_send, "dp", split_axis=1, concat_axis=0, tiled=True),
    )
    tile_tokens = gathered.reshape(tiles_here, TILE, full_width)
    gate_value = jnp.einsum(
        "tnd,dtc->tnc", tile_tokens, gate_cols, preferred_element_type=jnp.float32
    )
    up_value = jnp.einsum("tnd,dtc->tnc", tile_tokens, up_cols, preferred_element_type=jnp.float32)
    alive = (active.reshape(tiles_here, 1, CAP, 1) < blocks).astype(jnp.float32)
    alive_mask = jnp.broadcast_to(alive, (tiles_here, 1, CAP, BLOCK)).reshape(
        tiles_here, 1, CAP * BLOCK
    )
    upstream = out_grad.reshape(tiles_here, TILE, CAP * BLOCK).astype(jnp.float32)
    positive = jnp.maximum(gate_value, 0.0)
    gate_grad = (upstream * up_value * 2.0 * positive * alive_mask).astype(jnp.bfloat16)
    up_grad = (upstream * positive * positive * alive_mask).astype(jnp.bfloat16)
    partial_value = jnp.einsum(
        "tnc,dtc->tnd", gate_grad, gate_cols, preferred_element_type=jnp.float32
    )
    partial_value = partial_value + jnp.einsum(
        "tnc,dtc->tnd", up_grad, up_cols, preferred_element_type=jnp.float32
    )
    summed = lax.psum_scatter(
        partial_value.reshape(row_count, full_width).astype(jnp.bfloat16),
        "tensor",
        scatter_dimension=1,
        tiled=True,
    )
    row_slices = lax.all_to_all(gathered, "dp", split_axis=1, concat_axis=0, tiled=True)
    slices_tiled = row_slices.reshape(peer_count * tiles_here, TILE, rows_local)
    gate_all, up_all = (
        lax.all_gather(gate_grad, "dp", axis=0, tiled=True),
        lax.all_gather(up_grad, "dp", axis=0, tiled=True),
    )
    gate_terms = jnp.einsum(
        "tnr,tnc->rtc", slices_tiled, gate_all, preferred_element_type=jnp.float32
    ).astype(jnp.bfloat16)
    up_terms = jnp.einsum(
        "tnr,tnc->rtc", slices_tiled, up_all, preferred_element_type=jnp.float32
    ).astype(jnp.bfloat16)
    gate_terms = gate_terms.reshape(rows_local, peer_count * slot_count, BLOCK)
    up_terms = up_terms.reshape(rows_local, peer_count * slot_count, BLOCK)
    placing = (
        listed.reshape(peer_count * slot_count, 1) == jnp.arange(blocks, dtype=jnp.int32)[None, :]
    ).astype(jnp.bfloat16)
    gate_weight_grad = jnp.einsum(
        "rsk,sb->rbk", gate_terms, placing, preferred_element_type=jnp.float32
    )
    up_weight_grad = jnp.einsum(
        "rsk,sb->rbk", up_terms, placing, preferred_element_type=jnp.float32
    )
    gate_weight_grad = gate_weight_grad.reshape(rows_local, blocks * BLOCK).astype(jnp.bfloat16)
    up_weight_grad = up_weight_grad.reshape(rows_local, blocks * BLOCK).astype(jnp.bfloat16)
    return (summed, gate_weight_grad, up_weight_grad)


def solution(mesh):
    placed = (
        P("dp", "tensor"),
        P("dp", "tensor", None),
        P("dp", "tensor", None),
        P("dp", "tensor"),
        P("dp", "tensor"),
    )
    return jax.shard_map(
        per_device,
        mesh=mesh,
        in_specs=placed,
        out_specs=(P("dp", "tensor"), P("dp", "tensor"), P("dp", "tensor")),
        check_vma=False,
    )
```

profile of v0, /device:TPU:0, one launch (start us, length us, event | category | flops | bytes accessed | tf_op | source)
XLA Modules:
  0.0 549.0 jit_solution(14331622517996536747)
XLA Ops:
  7.2 23.3 %all_gather.12 = s32[16,1,2]{2,1,0:T(1,128)S(1)} all-gather(s32[1,1,2]{2,1,0:T(1,128)} %param.9), channel_id=1, replica_groups=mesh['dp'=16,'tensor'=2] {'dp'}, dimensions={0}, use_global_device_ids=true | all-gather | bytes 136 | tf_op jit(solution)/shard_map/all_gather | solution.py:18
  30.8 19.9 %copy.77 = bf16[512,14336]{0,1:T(8,128)(2,1)} copy(bf16[512,14336]{1,0:T(8,128)(2,1)} %param.10) | data formatting | bytes 29360128 | tf_op args[3]
  50.8 19.9 %copy.79 = bf16[512,112,128]{2,0,1:T(8,128)(2,1)} copy(bf16[512,112,128]{0,2,1:T(8,128)(2,1)} %bitcast.100) | data formatting | bytes 29360128 | tf_op jit(solution)/shard_map/reshape | solution.py:22
  70.7 19.9 %copy.71 = bf16[512,14336]{0,1:T(8,128)(2,1)} copy(bf16[512,14336]{1,0:T(8,128)(2,1)} %param.11) | data formatting | bytes 29360128 | tf_op args[4]
  90.6 19.9 %copy.73 = bf16[512,112,128]{2,0,1:T(8,128)(2,1)} copy(bf16[512,112,128]{0,2,1:T(8,128)(2,1)} %bitcast.101) | data formatting | bytes 29360128 | tf_op jit(solution)/shard_map/reshape | solution.py:25
  110.5 8.2 %gather_fusion.1 = bf16[32,512,128]{2,1,0:T(8,128)(2,1)} fusion(bf16[512,112,128]{2,0,1:T(8,128)(2,1)} %copy.79, s32[1024]{0:T(1024)S(1)} %pad_clamp_fusion), kind=kCustom, calls=%fused_computation.1.clone | custom fusion | bytes 8388736 | tf_op jit(solution)/shard_map/jit(_take)/gather | solution.py:22
  118.7 8.3 %gather_fusion = bf16[32,512,128]{2,1,0:T(8,128)(2,1)} fusion(bf16[512,112,128]{2,0,1:T(8,128)(2,1)} %copy.73, s32[1024]{0:T(1024)S(1)} %pad_clamp_fusion), kind=kCustom, calls=%fused_computation.clone | custom fusion | bytes 8388736 | tf_op jit(solution)/shard_map/jit(_take)/gather | solution.py:25
  127.0 5.2 select_bitcast_fusion.1
  132.2 2.8 copy.106
  135.0 4.5 all-to-all-start.1
  139.5 4.9 copy.107
  144.4 72.6 %all-to-all-done.1 = bf16[512,16,256]{2,0,1:T(8,128)(2,1)} async-done(((bf16[512,16,256]{2,0,1:T(8,128)(2,1)}), bf16[512,16,256]{2,0,1:T(8,128)(2,1)}, u32[]{:S(2)}, u32[]{:S(2)}) %all-to-all-start.1) | async-done | bytes 4194336 | tf_op jit(solution)/shard_map/all_to_all | solution.py:29
  217.0 19.8 %all-to-all-start = ((bf16[512,16,256]{2,0,1:T(8,128)(2,1)}), bf16[512,16,256]{2,0,1:T(8,128)(2,1)}, u32[]{:S(2)}, u32[]{:S(2)}) async-start(bf16[512,16,256]{2,0,1:T(8,128)(2,1)} %bitcast.107), calls=%async_computation | async-start | bytes 8388608 | tf_op jit(solution)/shard_map/all_to_all | solution.py:30
  239.6 58.2 %all-gather.6.cloned.1.call-done = bf16[256,8192]{0,1:T(8,128)(2,1)} async-done(((bf16[256,4096]{0,1:T(8,128)(2,1)}), bf16[256,8192]{0,1:T(8,128)(2,1)}) %all-gather.6.cloned.1.call-update) | async-done | bytes 4194320 | tf_op jit(solution)/shard_map/all_gather | solution.py:16
  297.8 5.4 fusion.22
  303.2 11.1 %all-to-all-done = bf16[512,16,256]{2,0,1:T(8,128)(2,1)} async-done(((bf16[512,16,256]{2,0,1:T(8,128)(2,1)}), bf16[512,16,256]{2,0,1:T(8,128)(2,1)}, u32[]{:S(2)}, u32[]{:S(2)}) %all-to-all-start) | async-done | bytes 4194336 | tf_op jit(solution)/shard_map/all_to_all | solution.py:30
  314.4 5.4 fusion.20
  320.5 6.4 %copy.81 = bf16[256,16,512]{2,0,1:T(8,128)(2,1)} copy(bf16[256,16,512]{0,2,1:T(8,128)(2,1)} %bitcast.104) | data formatting | bytes 8388608 | tf_op jit(solution)/shard_map/all_to_all | solution.py:57
  327.0 19.8 %all-to-all-start.2 = ((bf16[256,16,512]{2,0,1:T(8,128)(2,1)}), bf16[256,16,512]{2,0,1:T(8,128)(2,1)}, u32[]{:S(2)}, u32[]{:S(2)}) async-start(bf16[256,16,512]{2,0,1:T(8,128)(2,1)} %copy.81), calls=%async_computation.3 | async-start | bytes 8388608 | tf_op jit(solution)/shard_map/all_to_all | solution.py:57
  347.0 3.5 fusion.29
  350.6 5.6 %fusion = bf16[256,8192]{1,0:T(8,128)(2,1)} fusion(f32[256,8192]{1,0:T(8,128)S(1)} %fusion.29, bf16[256,256]{0,1:T(8,128)(2,1)S(1)} %copy-done.3, bf16[8192,256]{1,0:T(8,128)(2,1)} %bitcast.7), kind=kOutput, calls=%fused_computation.7 | convolution fusion | flops 1077936128 | bytes 16908288 | tf_op jit(solution)/shard_map/tnc,dtc->tnd/dot_general | solution.py:48
  357.5 65.8 %all-gather.8.cloned.1.call-done = bf16[4096,256]{0,1:T(8,128)(2,1)} async-done(((bf16[256,256]{0,1:T(8,128)(2,1)}), bf16[4096,256]{0,1:T(8,128)(2,1)}) %all-gather.8.cloned.1.call-update) | async-done | bytes 2097168 | tf_op jit(solution)/shard_map/all_gather | solution.py:60
  423.3 11.5 %all-to-all-done.2 = bf16[256,16,512]{2,0,1:T(8,128)(2,1)} async-done(((bf16[256,16,512]{2,0,1:T(8,128)(2,1)}), bf16[256,16,512]{2,0,1:T(8,128)(2,1)}, u32[]{:S(2)}, u32[]{:S(2)}) %all-to-all-start.2) | async-done | bytes 4194336 | tf_op jit(solution)/shard_map/all_to_all | solution.py:57
  434.9 6.1 %fusion.5 = bf16[16,256,512]{2,1,0:T(8,128)(2,1)} fusion(bf16[256,16,512]{2,0,1:T(8,128)(2,1)} %all-to-all-done.2, bf16[32,16,8,256]{3,2,1,0:T(8,128)(2,1)} %bitcast.113), kind=kOutput, calls=%fused_computation.16 | convolution fusion | flops 1075838976 | bytes 10485760 | tf_op jit(solution)/shard_map/tnr,tnc->rtc/dot_general | solution.py:63
  441.0 7.9 %copy.83 = bf16[512,32,128]{2,1,0:T(8,128)(2,1)} copy(bf16[512,32,128]{0,2,1:T(8,128)(2,1)} %bitcast.110) | data formatting | bytes 8388608 | tf_op jit(solution)/shard_map/reshape | solution.py:69
  448.9 27.4 %all-gather.10.cloned.1.call-done = bf16[4096,256]{0,1:T(8,128)(2,1)} async-done(((bf16[256,256]{0,1:T(8,128)(2,1)}), bf16[4096,256]{0,1:T(8,128)(2,1)}) %all-gather.10.cloned.1.call-update) | async-done | bytes 2097168 | tf_op jit(solution)/shard_map/all_gather | solution.py:61
  476.3 6.1 %fusion.8 = bf16[16,256,512]{2,1,0:T(8,128)(2,1)} fusion(bf16[256,16,512]{2,0,1:T(8,128)(2,1)} %all-to-all-done.2, bf16[32,16,8,256]{3,2,1,0:T(8,128)(2,1)} %bitcast.114), kind=kOutput, calls=%fused_computation.17 | convolution fusion | flops 1075838976 | bytes 10485760 | tf_op jit(solution)/shard_map/tnr,tnc->rtc/dot_general | solution.py:66
  482.4 8.0 %copy.85 = bf16[512,32,128]{2,1,0:T(8,128)(2,1)} copy(bf16[512,32,128]{0,2,1:T(8,128)(2,1)} %bitcast.109) | data formatting | bytes 8388608 | tf_op jit(solution)/shard_map/reshape | solution.py:70
  490.4 11.7 %convolution_convert_fusion = bf16[112,512,128]{2,0,1:T(8,128)(2,1)} fusion(bf16[512,32,128]{2,1,0:T(8,128)(2,1)} %copy.85, s32[32]{0:T(128)S(1)} %eq.15), kind=kOutput, calls=%fused_computation.5 | convolution fusion | flops 477105664 | bytes 18874496 | tf_op jit(solution)/shard_map/rsk,sb->rbk/dot_general | solution.py:77
  502.1 16.6 %copy.104 = bf16[64,8,112,128]{3,1,2,0:T(8,128)(2,1)} copy(bf16[64,8,112,128]{3,2,1,0:T(8,128)(2,1)} %bitcast.103) | data formatting | bytes 29360128
  518.7 7.4 %convolution_convert_fusion.1 = bf16[112,512,128]{2,0,1:T(8,128)(2,1)} fusion(bf16[512,32,128]{2,1,0:T(8,128)(2,1)S(1)} %copy-done, s32[32]{0:T(128)S(1)} %eq.15), kind=kOutput, calls=%fused_computation.6 | convolution fusion | flops 477105664 | bytes 18874496 | tf_op jit(solution)/shard_map/rsk,sb->rbk/dot_general | solution.py:74
  526.1 16.4 %copy.105 = bf16[64,8,112,128]{3,1,2,0:T(8,128)(2,1)} copy(bf16[64,8,112,128]{3,2,1,0:T(8,128)(2,1)} %bitcast.102) | data formatting | bytes 29360128
  (35 shorter events, 5.4 us)
Async XLA Ops:
  135.0 82.0 %all-to-all-start.1 = ((bf16[512,16,256]{2,0,1:T(8,128)(2,1)}), bf16[512,16,256]{2,0,1:T(8,128)(2,1)}, u32[]{:S(2)}, u32[]{:S(2)}) async-start(bf16[512,16,256]{2,0,1:T(8,128)(2,1)} %bitcast.108), calls=%async_computation.1 | async-start | bytes 8388608 | tf_op jit(solution)/shard_map/all_to_all | solution.py:29
  217.0 19.9 %copy-start.1 = (bf16[256,4096]{1,0:T(8,128)(2,1)S(1)}, bf16[256,4096]{1,0:T(8,128)(2,1)}, u32[]{:S(2)}) copy-start(bf16[256,4096]{1,0:T(8,128)(2,1)} %param.7) | copy-start | bytes 6291460
  217.0 97.3 %all-to-all-start = ((bf16[512,16,256]{2,0,1:T(8,128)(2,1)}), bf16[512,16,256]{2,0,1:T(8,128)(2,1)}, u32[]{:S(2)}, u32[]{:S(2)}) async-start(bf16[512,16,256]{2,0,1:T(8,128)(2,1)} %bitcast.107), calls=%async_computation | async-start | bytes 8388608 | tf_op jit(solution)/shard_map/all_to_all | solution.py:30
  236.8 2.6 copy-start.4
  236.8 2.7 copy-start.5
  236.8 61.0 %all-gather.6.cloned.1.call-start = ((), (), s32[]{:S(2)}) async-start(), calls=%async_computation.4 | async-start | bytes 6291456 | tf_op jit(solution)/shard_map/all_gather | solution.py:16
  239.4 184.0 %all-gather.8.cloned.1.call-start = ((), (), s32[]{:S(2)}) async-start(), calls=%async_computation.6 | async-start | bytes 2228224 | tf_op jit(solution)/shard_map/all_gather | solution.py:60
  319.8 156.5 %all-gather.10.cloned.1.call-start = ((), (), s32[]{:S(2)}) async-start(), calls=%async_computation.7 | async-start | bytes 2228224 | tf_op jit(solution)/shard_map/all_gather | solution.py:61
  327.0 20.1 %copy-start.2 = (bf16[256,256]{0,1:T(8,128)(2,1)S(1)}, bf16[256,256]{0,1:T(8,128)(2,1)}, u32[]{:S(2)}) copy-start(bf16[256,256]{0,1:T(8,128)(2,1)} %fusion.20) | copy-start | bytes 393220
  327.0 107.9 %all-to-all-start.2 = ((bf16[256,16,512]{2,0,1:T(8,128)(2,1)}), bf16[256,16,512]{2,0,1:T(8,128)(2,1)}, u32[]{:S(2)}, u32[]{:S(2)}) async-start(bf16[256,16,512]{2,0,1:T(8,128)(2,1)} %copy.81), calls=%async_computation.3 | async-start | bytes 8388608 | tf_op jit(solution)/shard_map/all_to_all | solution.py:57
  346.8 3.8 copy-start.3
  346.8 195.7 %reduce-scatter.2.cloned.1.call-start = ((), (), s32[]{:S(2)}) async-start(), calls=%async_computation.5 | async-start | bytes 6291456 | tf_op jit(solution)/shard_map/reduce_scatter | solution.py:51
  502.1 16.6 %copy-start = (bf16[512,32,128]{2,1,0:T(8,128)(2,1)S(1)}, bf16[512,32,128]{2,1,0:T(8,128)(2,1)}, u32[]{:S(2)}) copy-start(bf16[512,32,128]{2,1,0:T(8,128)(2,1)} %copy.83) | copy-start | bytes 12582916
Sparse Core Ops, SparseCore 0:
  239.8 58.0 all-gather.5
  319.9 103.3 all-gather.7
  426.1 50.1 all-gather.9
  479.0 53.4 reduce-scatter.1
where the time goes:
time: 552 us; the launch traced here: 549 us
  waiting for transfers between devices  247 us (45%)
  local copies, waits for them, and re-layouts  163 us (30%)
  matrix products  51.3 us (9%)
  starting transfers between devices  44.5 us (8%)
  blocking collectives  23.3 us (4%)
  between operations  13.9 us (3%)
  other arithmetic  5.91 us (1%)
    unnamed x18, local copies, waits for them, and re-layouts  75.5 us
    all_to_all x1, waiting for transfers between devices, per_device(): lax.all_to_all(gate_send, 'dp', split_axis=1, concat_axis=0, tiled=True)  72.6 us
    all_gather x1, waiting for transfers between devices, per_device(): lax.all_gather(gate_grad, 'dp', axis=0, tiled=True)  65.8 us
    all_gather x1, waiting for transfers between devices, per_device(): gathered = lax.all_gather(tokens, 'tensor', axis=1, tiled=True)  58.2 us
    all_gather x1, waiting for transfers between devices, per_device(): lax.all_gather(up_grad, 'dp', axis=0, tiled=True)  27.4 us
    all_gather x1, blocking collectives, per_device(): listed = lax.all_gather(active, 'dp', axis=0, tiled=True)  23.3 us
    reshape x1, local copies, waits for them, and re-layouts, per_device(): w_gate.reshape(rows_local, blocks, BLOCK)  19.9 us
    reshape x1, local copies, waits for them, and re-layouts, per_device(): w_up.reshape(rows_local, blocks, BLOCK)  19.9 us
  transfers between devices with their start and end apart: 7, of which 6 were waited for; matrix products, arithmetic and copies ran while one was open for 20% of the time, Pallas kernels for 0%

commit v1 on v0

--- a/solution.py
+++ b/solution.py
@@ -6,6 +6,19 @@
 BLOCK = 128
 TILE = 256
 CAP = 2
+
+
+def gather_around(shard, axis, dim):
+    ways = lax.axis_size(axis)
+    up = [(d, (d + 1) % ways) for d in range(ways)]
+    down = [(d, (d - 1) % ways) for d in range(ways)]
+    earlier, later = ([shard], [shard])
+    for _ in range(ways // 2):
+        earlier.append(lax.ppermute(earlier[-1], axis, up))
+    for _ in range((ways - 1) // 2):
+        later.append(lax.ppermute(later[-1], axis, down))
+    line = jnp.concatenate([*earlier[::-1], *later[1:]], axis=dim)
+    return jnp.roll(line, (lax.axis_index(axis) - ways // 2) * shard.shape[dim], axis=dim)
 
 
 def per_device(tokens, out_grad, active, w_gate, w_up):
@@ -57,7 +70,7 @@
     row_slices = lax.all_to_all(gathered, "dp", split_axis=1, concat_axis=0, tiled=True)
     slices_tiled = row_slices.reshape(peer_count * tiles_here, TILE, rows_local)
     gate_all, up_all = (
-        lax.all_gather(gate_grad, "dp", axis=0, tiled=True),
+        gather_around(gate_grad, "dp", 0),
         lax.all_gather(up_grad, "dp", axis=0, tiled=True),
     )
     gate_terms = jnp.einsum(

time: 552 us -> 583 us (1.056); the launches traced: 549 us -> 574 us
  starting transfers between devices: 44.5 us -> 80.7 us
  waiting for transfers between devices: 247 us -> 215 us
  local copies, waits for them, and re-layouts: 163 us -> 184 us
    ppermute x0 -> x15, waiting for transfers between devices: none -> 79.9 us  [the longest x8 79.8 us: gather_around(): earlier.append(lax.ppermute(earlier[-1], axis, up))]
    all_gather x1 -> x0, waiting for transfers between devices: 65.8 us -> none  [per_device(): lax.all_gather(gate_grad, 'dp', axis=0, tiled=True)]
    ppermute x0 -> x15, starting transfers between devices: none -> 32.3 us  [the longest x7 31.9 us: gather_around(): later.append(lax.ppermute(later[-1], axis, down))]
    all_gather x1, waiting for transfers between devices: 27.4 us -> 0.01 us  [per_device(): lax.all_gather(up_grad, 'dp', axis=0, tiled=True)]
    unnamed x18 -> x47, local copies, waits for them, and re-layouts: 75.5 us -> 95.9 us
    all_to_all x1, waiting for transfers between devices: 11.5 us -> 0.01 us  [per_device(): lax.all_to_all(gathered, 'dp', split_axis=1, concat_axis=0, tiled=True)]
    all_to_all x1, waiting for transfers between devices: 11.1 us -> 4.72 us  [per_device(): lax.all_to_all(up_send, 'dp', split_axis=1, concat_axis=0, tiled=True)]
  transfers between devices with their start and end apart: 7 -> 21, of which waited for: 6 -> 13; matrix products, arithmetic and copies ran while one was open for 20% -> 24% of each run, Pallas kernels for 0% -> 0%
where the time goes in v1:
time: 583 us; the launch traced here: 574 us
  waiting for transfers between devices  215 us (37%)
  local copies, waits for them, and re-layouts  184 us (32%)
  starting transfers between devices  80.7 us (14%)
  matrix products  50.7 us (9%)
  blocking collectives  23.3 us (4%)
  between operations  13.9 us (2%)
  other arithmetic  5.92 us (1%)
    unnamed x47, local copies, waits for them, and re-layouts  95.9 us
    ppermute x8, waiting for transfers between devices, gather_around(): earlier.append(lax.ppermute(earlier[-1], axis, up))  79.8 us
    all_to_all x1, waiting for transfers between devices, per_device(): lax.all_to_all(gate_send, 'dp', split_axis=1, concat_axis=0, tiled=True)  72.5 us
    all_gather x1, waiting for transfers between devices, per_device(): gathered = lax.all_gather(tokens, 'tensor', axis=1, tiled=True)  58.2 us
    ppermute x7, starting transfers between devices, gather_around(): later.append(lax.ppermute(later[-1], axis, down))  31.9 us
    all_to_all x1, starting transfers between devices, per_device(): lax.all_to_all(gathered, 'dp', split_axis=1, concat_axis=0, tiled=True)  23.9 us
    all_gather x1, blocking collectives, per_device(): listed = lax.all_gather(active, 'dp', axis=0, tiled=True)  23.3 us
    reshape x1, local copies, waits for them, and re-layouts, per_device(): w_gate.reshape(rows_local, blocks, BLOCK)  19.9 us
  transfers between devices with their start and end apart: 21, of which 13 were waited for; matrix products, arithmetic and copies ran while one was open for 24% of the time, Pallas kernels for 0%

profile of v1, /device:TPU:0, one launch (start us, length us, event | category | flops | bytes accessed | tf_op | source)
XLA Modules:
  0.0 573.7 jit_solution(8455184476655787836)
XLA Ops:
  7.2 23.3 %all_gather.9 = s32[16,1,2]{2,1,0:T(1,128)S(1)} all-gather(s32[1,1,2]{2,1,0:T(1,128)} %param.9), channel_id=1, replica_groups=mesh['dp'=16,'tensor'=2] {'dp'}, dimensions={0}, use_global_device_ids=true | all-gather | bytes 136 | tf_op jit(solution)/shard_map/all_gather | solution.py:31
  30.8 19.9 %copy.73 = bf16[512,14336]{0,1:T(8,128)(2,1)} copy(bf16[512,14336]{1,0:T(8,128)(2,1)} %param.10) | data formatting | bytes 29360128 | tf_op args[3]
  50.8 19.9 %copy.75 = bf16[512,112,128]{2,0,1:T(8,128)(2,1)} copy(bf16[512,112,128]{0,2,1:T(8,128)(2,1)} %bitcast.99) | data formatting | bytes 29360128 | tf_op jit(solution)/shard_map/reshape | solution.py:35
  70.7 19.9 %copy.67 = bf16[512,14336]{0,1:T(8,128)(2,1)} copy(bf16[512,14336]{1,0:T(8,128)(2,1)} %param.11) | data formatting | bytes 29360128 | tf_op args[4]
  90.6 19.9 %copy.69 = bf16[512,112,128]{2,0,1:T(8,128)(2,1)} copy(bf16[512,112,128]{0,2,1:T(8,128)(2,1)} %bitcast.100) | data formatting | bytes 29360128 | tf_op jit(solution)/shard_map/reshape | solution.py:38
  110.5 8.2 %gather_fusion.1 = bf16[32,512,128]{2,1,0:T(8,128)(2,1)} fusion(bf16[512,112,128]{2,0,1:T(8,128)(2,1)} %copy.75, s32[1024]{0:T(1024)S(1)} %pad_clamp_fusion), kind=kCustom, calls=%fused_computation.1.clone | custom fusion | bytes 8388736 | tf_op jit(solution)/shard_map/jit(_take)/gather | solution.py:35
  118.8 8.3 %gather_fusion = bf16[32,512,128]{2,1,0:T(8,128)(2,1)} fusion(bf16[512,112,128]{2,0,1:T(8,128)(2,1)} %copy.69, s32[1024]{0:T(1024)S(1)} %pad_clamp_fusion), kind=kCustom, calls=%fused_computation.clone | custom fusion | bytes 8388736 | tf_op jit(solution)/shard_map/jit(_take)/gather | solution.py:38
  127.0 5.2 select_bitcast_fusion.1
  135.0 4.6 all-to-all-start.1
  139.6 4.9 copy.97
  144.5 72.5 %all-to-all-done.1 = bf16[512,16,256]{2,0,1:T(8,128)(2,1)} async-done(((bf16[512,16,256]{2,0,1:T(8,128)(2,1)}), bf16[512,16,256]{2,0,1:T(8,128)(2,1)}, u32[]{:S(2)}, u32[]{:S(2)}) %all-to-all-start.1) | async-done | bytes 4194336 | tf_op jit(solution)/shard_map/all_to_all | solution.py:42
  217.1 19.8 %all-to-all-start = ((bf16[512,16,256]{2,0,1:T(8,128)(2,1)}), bf16[512,16,256]{2,0,1:T(8,128)(2,1)}, u32[]{:S(2)}, u32[]{:S(2)}) async-start(bf16[512,16,256]{2,0,1:T(8,128)(2,1)} %bitcast.106), calls=%async_computation | async-start | bytes 8388608 | tf_op jit(solution)/shard_map/all_to_all | solution.py:43
  239.7 58.2 %all-gather.4.cloned.1.call-done = bf16[256,8192]{0,1:T(8,128)(2,1)} async-done(((bf16[256,4096]{0,1:T(8,128)(2,1)}), bf16[256,8192]{0,1:T(8,128)(2,1)}) %all-gather.4.cloned.1.call-update) | async-done | bytes 4194320 | tf_op jit(solution)/shard_map/all_gather | solution.py:29
  297.9 5.4 fusion.21
  303.3 6.4 %copy.77 = bf16[256,16,512]{2,0,1:T(8,128)(2,1)} copy(bf16[256,16,512]{0,2,1:T(8,128)(2,1)} %bitcast.103) | data formatting | bytes 8388608 | tf_op jit(solution)/shard_map/all_to_all | solution.py:70
  309.7 4.7 all-to-all-done
  314.4 23.9 %all-to-all-start.2 = ((bf16[256,16,512]{2,0,1:T(8,128)(2,1)}), bf16[256,16,512]{2,0,1:T(8,128)(2,1)}, u32[]{:S(2)}, u32[]{:S(2)}) async-start(bf16[256,16,512]{2,0,1:T(8,128)(2,1)} %copy.77), calls=%async_computation.3 | async-start | bytes 8388608 | tf_op jit(solution)/shard_map/all_to_all | solution.py:70
  338.4 4.8 fusion.19
  346.8 5.7 fusion
  352.9 63.1 %collective-permute-done = bf16[1,256,256]{1,2,0:T(8,128)(2,1)S(1)} collective-permute-done((bf16[1,256,256]{1,2,0:T(8,128)(2,1)S(1)}, bf16[1,256,256]{1,2,0:T(8,128)(2,1)S(1)}, u32[]{:S(2)}, u32[]{:S(2)}) %collective-permute-start) | collective-permute-done | bytes 131104 | tf_op jit(solution)/shard_map/ppermute | solution.py:17
  430.4 4.6 collective-permute-start.10
  437.6 4.7 collective-permute-start.11
  444.8 4.6 collective-permute-start.12
  451.9 4.6 collective-permute-start.13
  487.3 6.1 %fusion.8 = bf16[16,256,512]{2,1,0:T(8,128)(2,1)} fusion(bf16[256,16,512]{2,0,1:T(8,128)(2,1)} %all-to-all-done.2, bf16[32,16,8,256]{3,2,1,0:T(8,128)(2,1)} %bitcast.114), kind=kOutput, calls=%fused_computation.17 | convolution fusion | flops 1075838976 | bytes 10485760 | tf_op jit(solution)/shard_map/tnr,tnc->rtc/dot_general | solution.py:79
  493.4 7.9 %copy.80 = bf16[512,32,128]{2,1,0:T(8,128)(2,1)} copy(bf16[512,32,128]{0,2,1:T(8,128)(2,1)} %bitcast.109) | data formatting | bytes 8388608 | tf_op jit(solution)/shard_map/reshape | solution.py:83
  501.3 6.1 %fusion.5 = bf16[16,256,512]{2,1,0:T(8,128)(2,1)} fusion(bf16[256,16,512]{2,0,1:T(8,128)(2,1)} %all-to-all-done.2, bf16[32,256,256]{1,2,0:T(8,128)(2,1)} %constant_dynamic-update-slice_fusion, s32[]{:T(128)S(6)} %select_n.21), kind=kOutput, calls=%fused_computation.16 | convolution fusion | flops 1075838976 | bytes 10485764 | tf_op jit(solution)/shard_map/tnr,tnc->rtc/dot_general | solution.py:76
  507.4 7.8 %copy.78 = bf16[512,32,128]{2,1,0:T(8,128)(2,1)} copy(bf16[512,32,128]{0,2,1:T(8,128)(2,1)} %bitcast.108) | data formatting | bytes 8388608 | tf_op jit(solution)/shard_map/reshape | solution.py:82
  515.2 11.7 %convolution_convert_fusion.1 = bf16[112,512,128]{2,0,1:T(8,128)(2,1)} fusion(bf16[512,32,128]{2,1,0:T(8,128)(2,1)} %copy.78, s32[32]{0:T(128)S(1)} %eq.18), kind=kOutput, calls=%fused_computation.6 | convolution fusion | flops 477105664 | bytes 18874496 | tf_op jit(solution)/shard_map/rsk,sb->rbk/dot_general | solution.py:87
  526.9 16.5 %copy.95 = bf16[64,8,112,128]{3,1,2,0:T(8,128)(2,1)} copy(bf16[64,8,112,128]{3,2,1,0:T(8,128)(2,1)} %bitcast.102) | data formatting | bytes 29360128
  543.4 7.4 %convolution_convert_fusion = bf16[112,512,128]{2,0,1:T(8,128)(2,1)} fusion(bf16[512,32,128]{2,1,0:T(8,128)(2,1)S(1)} %copy-done, s32[32]{0:T(128)S(1)} %eq.18), kind=kOutput, calls=%fused_computation.5 | convolution fusion | flops 477105664 | bytes 18874496 | tf_op jit(solution)/shard_map/rsk,sb->rbk/dot_general | solution.py:90
  550.8 16.3 %copy.94 = bf16[64,8,112,128]{3,1,2,0:T(8,128)(2,1)} copy(bf16[64,8,112,128]{3,2,1,0:T(8,128)(2,1)} %bitcast.101) | data formatting | bytes 29360128
  (92 shorter events, 62.7 us)
Async XLA Ops:
  135.0 82.0 %all-to-all-start.1 = ((bf16[512,16,256]{2,0,1:T(8,128)(2,1)}), bf16[512,16,256]{2,0,1:T(8,128)(2,1)}, u32[]{:S(2)}, u32[]{:S(2)}) async-start(bf16[512,16,256]{2,0,1:T(8,128)(2,1)} %bitcast.107), calls=%async_computation.1 | async-start | bytes 8388608 | tf_op jit(solution)/shard_map/all_to_all | solution.py:42
  217.1 19.9 %copy-start.1 = (bf16[256,4096]{1,0:T(8,128)(2,1)S(1)}, bf16[256,4096]{1,0:T(8,128)(2,1)}, u32[]{:S(2)}) copy-start(bf16[256,4096]{1,0:T(8,128)(2,1)} %param.7) | copy-start | bytes 6291460
  217.1 97.4 %all-to-all-start = ((bf16[512,16,256]{2,0,1:T(8,128)(2,1)}), bf16[512,16,256]{2,0,1:T(8,128)(2,1)}, u32[]{:S(2)}, u32[]{:S(2)}) async-start(bf16[512,16,256]{2,0,1:T(8,128)(2,1)} %bitcast.106), calls=%async_computation | async-start | bytes 8388608 | tf_op jit(solution)/shard_map/all_to_all | solution.py:43
  236.9 2.6 copy-start.3
  236.9 2.7 copy-start.4
  236.9 61.0 %all-gather.4.cloned.1.call-start = ((), (), s32[]{:S(2)}) async-start(), calls=%async_computation.4 | async-start | bytes 6291456 | tf_op jit(solution)/shard_map/all_gather | solution.py:29
  239.4 247.8 %all-gather.6.cloned.1.call-start = ((), (), s32[]{:S(2)}) async-start(), calls=%async_computation.6 | async-start | bytes 2228224 | tf_op jit(solution)/shard_map/all_gather | solution.py:74
  314.4 172.8 %all-to-all-start.2 = ((bf16[256,16,512]{2,0,1:T(8,128)(2,1)}), bf16[256,16,512]{2,0,1:T(8,128)(2,1)}, u32[]{:S(2)}, u32[]{:S(2)}) async-start(bf16[256,16,512]{2,0,1:T(8,128)(2,1)} %copy.77), calls=%async_computation.3 | async-start | bytes 8388608 | tf_op jit(solution)/shard_map/all_to_all | solution.py:70
  338.4 228.8 %reduce-scatter.2.cloned.1.call-start = ((), (), s32[]{:S(2)}) async-start(), calls=%async_computation.5 | async-start | bytes 6291456 | tf_op jit(solution)/shard_map/reduce_scatter | solution.py:64
  343.2 3.5 copy-start.2
  352.5 63.4 %collective-permute-start = (bf16[1,256,256]{1,2,0:T(8,128)(2,1)S(1)}, bf16[1,256,256]{1,2,0:T(8,128)(2,1)S(1)}, u32[]{:S(2)}, u32[]{:S(2)}) collective-permute-start(bf16[1,256,256]{1,2,0:T(8,128)(2,1)S(1)} %bitcast.112), channel_id=1, source_target_pairs={{0,2},{2,4},{4,6},{6,8},{8,10},{10,12},{12,14},{14,16},{16,18},{18... | collective-permute-start | bytes 393224 | tf_op jit(solution)/shard_map/ppermute | solution.py:17
  415.9 7.2 %collective-permute-start.1 = (bf16[1,256,256]{1,2,0:T(8,128)(2,1)S(1)}, bf16[1,256,256]{1,2,0:T(8,128)(2,1)S(1)}, u32[]{:S(2)}, u32[]{:S(2)}) collective-permute-start(bf16[1,256,256]{1,2,0:T(8,128)(2,1)S(1)} %collective-permute-done), channel_id=1, source_target_pairs={{0,2},{2,4},{4,6},{6,8},{8,10},{10,12},{12,14},{14,16},{16,18},{18... | collective-permute-start | bytes 393224 | tf_op jit(solution)/shard_map/ppermute | solution.py:17
  415.9 7.2 %collective-permute-start.8 = (bf16[1,256,256]{1,2,0:T(8,128)(2,1)S(1)}, bf16[1,256,256]{1,2,0:T(8,128)(2,1)S(1)}, u32[]{:S(2)}, u32[]{:S(2)}) collective-permute-start(bf16[1,256,256]{1,2,0:T(8,128)(2,1)S(1)} %bitcast.113), channel_id=1, source_target_pairs={{0,30},{2,0},{4,2},{6,4},{8,6},{10,8},{12,10},{14,12},{16,14},{18,... | collective-permute-start | bytes 393224 | tf_op jit(solution)/shard_map/ppermute | solution.py:19
  423.2 7.2 %collective-permute-start.2 = (bf16[1,256,256]{1,2,0:T(8,128)(2,1)S(1)}, bf16[1,256,256]{1,2,0:T(8,128)(2,1)S(1)}, u32[]{:S(2)}, u32[]{:S(2)}) collective-permute-start(bf16[1,256,256]{1,2,0:T(8,128)(2,1)S(1)} %collective-permute-done.1), channel_id=1, source_target_pairs={{0,2},{2,4},{4,6},{6,8},{8,10},{10,12},{12,14},{14,16},{16,18},{18... | collective-permute-start | bytes 393224 | tf_op jit(solution)/shard_map/ppermute | solution.py:17
  423.2 7.2 %collective-permute-start.9 = (bf16[1,256,256]{1,2,0:T(8,128)(2,1)S(1)}, bf16[1,256,256]{1,2,0:T(8,128)(2,1)S(1)}, u32[]{:S(2)}, u32[]{:S(2)}) collective-permute-start(bf16[1,256,256]{1,2,0:T(8,128)(2,1)S(1)} %collective-permute-done.8), channel_id=1, source_target_pairs={{0,30},{2,0},{4,2},{6,4},{8,6},{10,8},{12,10},{14,12},{16,14},{18,... | collective-permute-start | bytes 393224 | tf_op jit(solution)/shard_map/ppermute | solution.py:19
  430.4 7.2 %collective-permute-start.3 = (bf16[1,256,256]{1,2,0:T(8,128)(2,1)S(1)}, bf16[1,256,256]{1,2,0:T(8,128)(2,1)S(1)}, u32[]{:S(2)}, u32[]{:S(2)}) collective-permute-start(bf16[1,256,256]{1,2,0:T(8,128)(2,1)S(1)} %collective-permute-done.2), channel_id=1, source_target_pairs={{0,2},{2,4},{4,6},{6,8},{8,10},{10,12},{12,14},{14,16},{16,18},{18... | collective-permute-start | bytes 393224 | tf_op jit(solution)/shard_map/ppermute | solution.py:17
  430.4 7.2 %collective-permute-start.10 = (bf16[1,256,256]{1,2,0:T(8,128)(2,1)S(1)}, bf16[1,256,256]{1,2,0:T(8,128)(2,1)S(1)}, u32[]{:S(2)}, u32[]{:S(2)}) collective-permute-start(bf16[1,256,256]{1,2,0:T(8,128)(2,1)S(1)} %collective-permute-done.9), channel_id=1, source_target_pairs={{0,30},{2,0},{4,2},{6,4},{8,6},{10,8},{12,10},{14,12},{16,14},{18,... | collective-permute-start | bytes 393224 | tf_op jit(solution)/shard_map/ppermute | solution.py:19
  437.5 7.2 %collective-permute-start.4 = (bf16[1,256,256]{1,2,0:T(8,128)(2,1)S(1)}, bf16[1,256,256]{1,2,0:T(8,128)(2,1)S(1)}, u32[]{:S(2)}, u32[]{:S(2)}) collective-permute-start(bf16[1,256,256]{1,2,0:T(8,128)(2,1)S(1)} %collective-permute-done.3), channel_id=1, source_target_pairs={{0,2},{2,4},{4,6},{6,8},{8,10},{10,12},{12,14},{14,16},{16,18},{18... | collective-permute-start | bytes 393224 | tf_op jit(solution)/shard_map/ppermute | solution.py:17
  437.6 7.3 %collective-permute-start.11 = (bf16[1,256,256]{1,2,0:T(8,128)(2,1)S(1)}, bf16[1,256,256]{1,2,0:T(8,128)(2,1)S(1)}, u32[]{:S(2)}, u32[]{:S(2)}) collective-permute-start(bf16[1,256,256]{1,2,0:T(8,128)(2,1)S(1)} %collective-permute-done.10), channel_id=1, source_target_pairs={{0,30},{2,0},{4,2},{6,4},{8,6},{10,8},{12,10},{14,12},{16,14},{18,... | collective-permute-start | bytes 393224 | tf_op jit(solution)/shard_map/ppermute | solution.py:19
  444.7 7.1 %collective-permute-start.5 = (bf16[1,256,256]{1,2,0:T(8,128)(2,1)S(1)}, bf16[1,256,256]{1,2,0:T(8,128)(2,1)S(1)}, u32[]{:S(2)}, u32[]{:S(2)}) collective-permute-start(bf16[1,256,256]{1,2,0:T(8,128)(2,1)S(1)} %collective-permute-done.4), channel_id=1, source_target_pairs={{0,2},{2,4},{4,6},{6,8},{8,10},{10,12},{12,14},{14,16},{16,18},{18... | collective-permute-start | bytes 393224 | tf_op jit(solution)/shard_map/ppermute | solution.py:17
  444.8 7.1 %collective-permute-start.12 = (bf16[1,256,256]{1,2,0:T(8,128)(2,1)S(1)}, bf16[1,256,256]{1,2,0:T(8,128)(2,1)S(1)}, u32[]{:S(2)}, u32[]{:S(2)}) collective-permute-start(bf16[1,256,256]{1,2,0:T(8,128)(2,1)S(1)} %collective-permute-done.11), channel_id=1, source_target_pairs={{0,30},{2,0},{4,2},{6,4},{8,6},{10,8},{12,10},{14,12},{16,14},{18,... | collective-permute-start | bytes 393224 | tf_op jit(solution)/shard_map/ppermute | solution.py:19
  451.8 7.1 %collective-permute-start.6 = (bf16[1,256,256]{1,2,0:T(8,128)(2,1)S(1)}, bf16[1,256,256]{1,2,0:T(8,128)(2,1)S(1)}, u32[]{:S(2)}, u32[]{:S(2)}) collective-permute-start(bf16[1,256,256]{1,2,0:T(8,128)(2,1)S(1)} %collective-permute-done.5), channel_id=1, source_target_pairs={{0,2},{2,4},{4,6},{6,8},{8,10},{10,12},{12,14},{14,16},{16,18},{18... | collective-permute-start | bytes 393224 | tf_op jit(solution)/shard_map/ppermute | solution.py:17
  451.9 8.3 %collective-permute-start.13 = (bf16[1,256,256]{1,2,0:T(8,128)(2,1)S(1)}, bf16[1,256,256]{1,2,0:T(8,128)(2,1)S(1)}, u32[]{:S(2)}, u32[]{:S(2)}) collective-permute-start(bf16[1,256,256]{1,2,0:T(8,128)(2,1)S(1)} %collective-permute-done.12), channel_id=1, source_target_pairs={{0,30},{2,0},{4,2},{6,4},{8,6},{10,8},{12,10},{14,12},{16,14},{18,... | collective-permute-start | bytes 393224 | tf_op jit(solution)/shard_map/ppermute | solution.py:19
  458.9 7.1 %collective-permute-start.7 = (bf16[1,256,256]{1,2,0:T(8,128)(2,1)S(1)}, bf16[1,256,256]{1,2,0:T(8,128)(2,1)S(1)}, u32[]{:S(2)}, u32[]{:S(2)}) collective-permute-start(bf16[1,256,256]{1,2,0:T(8,128)(2,1)S(1)} %collective-permute-done.6), channel_id=1, source_target_pairs={{0,2},{2,4},{4,6},{6,8},{8,10},{10,12},{12,14},{14,16},{16,18},{18... | collective-permute-start | bytes 393224 | tf_op jit(solution)/shard_map/ppermute | solution.py:17
  460.2 15.8 %collective-permute-start.14 = (bf16[1,256,256]{1,2,0:T(8,128)(2,1)S(1)}, bf16[1,256,256]{1,2,0:T(8,128)(2,1)S(1)}, u32[]{:S(2)}, u32[]{:S(2)}) collective-permute-start(bf16[1,256,256]{1,2,0:T(8,128)(2,1)S(1)} %collective-permute-done.13), channel_id=1, source_target_pairs={{0,30},{2,0},{4,2},{6,4},{8,6},{10,8},{12,10},{14,12},{16,14},{18,... | collective-permute-start | bytes 393224 | tf_op jit(solution)/shard_map/ppermute | solution.py:19
  526.9 16.5 %copy-start = (bf16[512,32,128]{2,1,0:T(8,128)(2,1)S(1)}, bf16[512,32,128]{2,1,0:T(8,128)(2,1)}, u32[]{:S(2)}) copy-start(bf16[512,32,128]{2,1,0:T(8,128)(2,1)} %copy.80) | copy-start | bytes 12582916
Sparse Core Ops, SparseCore 0:
  239.8 58.0 all-gather.3
  303.4 69.8 all-gather.5
  376.2 53.3 reduce-scatter.1
